TPU v7x, 512 devices: a whole 4x4x16 slice. The times are simulated.
512 devices in a mesh: rows: 64 (over z, y), cols: 8 (over x, core).
Axes of the slice: x: 4, y: 4, z: 16, core: 2. Of those that a mesh axis runs over, the one named last changes fastest.
Arguments:
- lower_pivot: bfloat16 [4, 2048, 4, 2048], P(None, 'rows', None, 'cols'), may hold values from -0.0625 to 0.0625
- lower_rest: bfloat16 [98304, 4, 2048], P('rows', None, 'cols'), may hold values from -0.0625 to 0.0625
- diag_inverse: bfloat16 [4, 2048, 2048], P(None, 'cols', 'rows'), may hold values from -0.125 to 0.125
- rhs_pivot: bfloat16 [4, 2048, 512], P(None, 'rows', 'cols'), may hold values from -6 to 6
- rhs_rest: bfloat16 [512, 98304], P('cols', 'rows'), may hold values from -6 to 6
Outputs:
- solution: bfloat16 [4, 2048, 512], P(None, 'cols')
- remainder: bfloat16 [512, 98304], P('cols', 'rows')
All inputs are finite; a program needn't handle non-finite values.
Results may differ from a plain program's by a relative error of at most 0.017.
Values may be sent and summed in bfloat16 or wider, within the bound.
A program may use at most 64 MiB of HBM per device.

v0:
```python
import jax
import jax.numpy as jnp
from jax import lax
from jax.sharding import PartitionSpec as P


def per_device(lower_pivot, lower_rest, diag_inverse, rhs_pivot, rhs_rest):
    block_count = lower_pivot.shape[0]
    pivot_rows = lower_pivot.shape[1]
    share_width = lower_pivot.shape[3]
    sides_share = rhs_pivot.shape[2]
    sides_total = sides_share * lax.axis_size("cols")
    rest_rows = lower_rest.shape[0]
    col_offset = lax.axis_index("cols") * sides_share
    solved = []
    for step_index in range(block_count):
        partials = jnp.zeros((pivot_rows, sides_total), jnp.float32)
        partials = lax.dynamic_update_slice(
            partials, rhs_pivot[step_index].astype(jnp.float32), (jnp.int32(0), col_offset)
        )
        if step_index > 0:
            factor_part = lower_pivot[step_index, :, :step_index, :].reshape(
                pivot_rows, step_index * share_width
            )
            known_part = jnp.concatenate(solved, axis=0)
            partials = partials - jnp.dot(
                factor_part, known_part, preferred_element_type=jnp.float32
            )
        residual = lax.psum(partials.astype(jnp.bfloat16), "cols")
        product = jnp.dot(diag_inverse[step_index], residual, preferred_element_type=jnp.float32)
        solved_block = lax.psum(product, "rows").astype(jnp.bfloat16)
        solved.append(solved_block)
    solution = jnp.stack(solved)
    flat_solution = solution.reshape(block_count * share_width, sides_total)
    flat_lower = lower_rest.reshape(rest_rows, block_count * share_width)
    total_sum = lax.psum_scatter(
        lax.dot_general(
            flat_solution, flat_lower, (((0,), (1,)), ((), ())), preferred_element_type=jnp.float32
        ).astype(jnp.bfloat16),
        "cols",
        scatter_dimension=0,
        tiled=True,
    ).astype(jnp.float32)
    remainder = (rhs_rest.astype(jnp.float32) - total_sum).astype(jnp.bfloat16)
    return (solution, remainder)


def solution(mesh):
    placed = (
        P(None, "rows", None, "cols"),
        P("rows", None, "cols"),
        P(None, "cols", "rows"),
        P(None, "rows", "cols"),
        P("cols", "rows"),
    )
    return jax.shard_map(
        per_device,
        mesh=mesh,
        in_specs=placed,
        out_specs=(P(None, "cols", None), P("cols", "rows")),
        check_vma=False,
    )
```

profile of v0, /device:TPU:8, one launch (start us, length us, event | category | flops | bytes accessed | tf_op | source)
XLA Modules:
  0.0 1294.9 jit_solution(7046899199717933439)
XLA Ops:
  7.2 0.0 copy-start
  7.2 0.0 reduce-scatter.2.cloned.1.call-start
  7.2 1.6 slice.36
  8.8 1.5 slice.39
  10.3 0.9 slice.42
  11.2 1.4 bitcast_convert_fusion.3
  12.6 0.3 dynamic_update_slice.12
  12.9 25.7 %psum.56 = bf16[32,512]{1,0:T(8,128)(2,1)S(1)} all-reduce(bf16[32,512]{1,0:T(8,128)(2,1)S(1)} %convert_element_type.62), channel_id=1, replica_groups=mesh['rows'=64,'cols'=8] {'cols'}, use_global_device_ids=true, to_apply=%region_0.0 | all-reduce | flops 16384 | bytes 65536 | tf_op jit(solution)/shard_map/psum | solution.py:29
  38.6 1.8 convolution_bitcast_fusion.4
  40.3 284.2 %all-reduce.4 = bf16[256,512]{0,1:T(8,128)(2,1)S(1)} all-reduce(f32[256,512]{0,1:T(8,128)} %convolution_bitcast_fusion.4), channel_id=1, replica_groups=mesh['rows'=64,'cols'=8] {'rows'}, use_global_device_ids=true, to_apply=%region_1.0 | all-reduce | flops 131072 | bytes 786432 | tf_op jit(solution)/shard_map/psum | solution.py:31
  324.5 0.9 dynamic_update_slice.13
  325.4 1.6 fusion.7
  327.0 24.2 %psum.58 = bf16[32,512]{1,0:T(8,128)(2,1)S(1)} all-reduce(bf16[32,512]{1,0:T(8,128)(2,1)} %fusion.7), channel_id=1, replica_groups=mesh['rows'=64,'cols'=8] {'cols'}, use_global_device_ids=true, to_apply=%region_2.0 | all-reduce | flops 16384 | bytes 65536 | tf_op jit(solution)/shard_map/psum | solution.py:29
  351.1 1.8 convolution_bitcast_fusion.3
  352.9 280.2 %all-reduce.5 = bf16[256,512]{0,1:T(8,128)(2,1)} all-reduce(f32[256,512]{0,1:T(8,128)} %convolution_bitcast_fusion.3), channel_id=1, replica_groups=mesh['rows'=64,'cols'=8] {'rows'}, use_global_device_ids=true, to_apply=%region_3.0 | all-reduce | flops 131072 | bytes 786432 | tf_op jit(solution)/shard_map/psum | solution.py:31
  633.1 1.4 copy.13
  634.5 0.9 dynamic_update_slice.14
  635.4 1.8 fusion.9
  637.2 24.2 %psum.60 = bf16[32,512]{1,0:T(8,128)(2,1)S(1)} all-reduce(bf16[32,512]{1,0:T(8,128)(2,1)} %fusion.9), channel_id=1, replica_groups=mesh['rows'=64,'cols'=8] {'cols'}, use_global_device_ids=true, to_apply=%region_4.0 | all-reduce | flops 16384 | bytes 65536 | tf_op jit(solution)/shard_map/psum | solution.py:29
  661.4 1.8 convolution_bitcast_fusion.2
  663.1 277.9 %all-reduce.6 = bf16[256,512]{0,1:T(8,128)(2,1)} all-reduce(f32[256,512]{0,1:T(8,128)} %convolution_bitcast_fusion.2), channel_id=1, replica_groups=mesh['rows'=64,'cols'=8] {'rows'}, use_global_device_ids=true, to_apply=%region_5.0 | all-reduce | flops 131072 | bytes 786432 | tf_op jit(solution)/shard_map/psum | solution.py:31
  941.1 0.3 dynamic_update_slice.15
  941.4 1.4 fusion.8
  942.8 23.6 %psum.62 = bf16[32,512]{1,0:T(8,128)(2,1)S(1)} all-reduce(bf16[32,512]{1,0:T(8,128)(2,1)S(1)} %fusion.8), channel_id=1, replica_groups=mesh['rows'=64,'cols'=8] {'cols'}, use_global_device_ids=true, to_apply=%region_6.0 | all-reduce | flops 16384 | bytes 65536 | tf_op jit(solution)/shard_map/psum | solution.py:29
  966.4 1.8 convolution_bitcast_fusion.1
  968.2 279.9 %all-reduce.7 = bf16[256,512]{0,1:T(8,128)(2,1)} all-reduce(f32[256,512]{0,1:T(8,128)} %convolution_bitcast_fusion.1), channel_id=1, replica_groups=mesh['rows'=64,'cols'=8] {'rows'}, use_global_device_ids=true, to_apply=%region_7.0 | all-reduce | flops 131072 | bytes 786432 | tf_op jit(solution)/shard_map/psum | solution.py:31
  1248.1 0.0 copy-done
  1248.1 4.1 fusion.1
  1252.2 0.0 reduce-scatter.2.cloned.1.call-update
  1252.2 2.2 pad_maximum_fusion
  1254.4 0.0 copy-start.1
  1254.4 2.3 copy.11
  1256.7 29.6 %reduce-scatter.2.cloned.1.call-done = bf16[64,1536]{1,0:T(8,128)(2,1)} async-done(((bf16[512,1536]{1,0:T(8,128)(2,1)}), bf16[64,1536]{1,0:T(8,128)(2,1)}) %reduce-scatter.2.cloned.1.call-update) | async-done | bytes 196624 | tf_op jit(solution)/shard_map/reduce_scatter | solution.py:36
  1286.4 0.0 copy-done.1
  1286.4 1.6 subtract_convert_fusion
  (6 shorter events, 0.0 us)
Async XLA Ops:
  7.2 1240.9 %copy-start = (bf16[1536,4,256]{2,1,0:T(4,128)(2,1)S(1)}, bf16[1536,4,256]{2,1,0:T(4,128)(2,1)}, u32[]{:S(2)}) copy-start(bf16[1536,4,256]{2,1,0:T(4,128)(2,1)} %param.6) | copy-start | bytes 9437188
  7.2 1279.2 %reduce-scatter.2.cloned.1.call-start = ((), (), s32[]{:S(2)}) async-start(), calls=%async_computation.1 | async-start | bytes 1769472 | tf_op jit(solution)/shard_map/reduce_scatter | solution.py:36
  1254.4 31.9 %copy-start.1 = (bf16[64,1536]{1,0:T(8,128)(2,1)S(1)}, bf16[64,1536]{1,0:T(8,128)(2,1)}, u32[]{:S(2)}) copy-start(bf16[64,1536]{1,0:T(8,128)(2,1)} %param.9) | copy-start | bytes 589828
Sparse Core Ops, SparseCore 0:
  1252.3 33.9 reduce-scatter.1
where the time goes:
time: 1300 us; the launch traced here: 1290 us
  blocking collectives  1220 us (94%)
  waiting for transfers between devices  29.6 us (2%)
  matrix products  15.9 us (1%)
  between operations  14.1 us (1%)
    psum x4, blocking collectives, per_device(): solved_block = lax.psum(product, 'rows').astype(jnp.bfloat16)  1120 us
    psum x4, blocking collectives, per_device(): residual = lax.psum(partials.astype(jnp.bfloat16), 'cols')  97.6 us
    reduce_scatter x1, waiting for transfers between devices, per_device(): lax.psum_scatter(lax.dot_general(flat_solution, flat_lower, (((0,), (1,))...  29.6 us
  transfers between devices with their start and end apart: 1, of which 1 were waited for; matrix products, arithmetic and copies ran while one was open for 0% of the time, Pallas kernels for 0%

commit v1 on v0

--- a/solution.py
+++ b/solution.py
@@ -26,7 +26,9 @@
             partials = partials - jnp.dot(
                 factor_part, known_part, preferred_element_type=jnp.float32
             )
-        residual = lax.psum(partials.astype(jnp.bfloat16), "cols")
+        block = partials.astype(jnp.bfloat16)
+        parts = lax.all_gather(block, "cols")
+        residual = jnp.sum(parts, axis=0)
         product = jnp.dot(diag_inverse[step_index], residual, preferred_element_type=jnp.float32)
         solved_block = lax.psum(product, "rows").astype(jnp.bfloat16)
         solved.append(solved_block)

time: 1300 us -> 1260 us (0.969)
  blocking collectives: 1220 us -> 1180 us
    psum x4 -> x0, blocking collectives: 97.6 us -> none  [per_device(): residual = lax.psum(partials.astype(jnp.bfloat16), 'cols')]
    all_gather x0 -> x4, blocking collectives: none -> 54.9 us  [per_device(): parts = lax.all_gather(block, 'cols')]
where the time goes in v1:
time: 1260 us
  blocking collectives  1180 us (94%)
  waiting for transfers between devices  31.3 us (2%)
  matrix products  14.7 us (1%)
  between operations  14.2 us (1%)
    psum x4, blocking collectives, per_device(): solved_block = lax.psum(product, 'rows').astype(jnp.bfloat16)  1120 us
    all_gather x4, blocking collectives, per_device(): parts = lax.all_gather(block, 'cols')  54.9 us
    reduce_scatter x1, waiting for transfers between devices, per_device(): lax.psum_scatter(lax.dot_general(flat_solution, flat_lower, (((0,), (1,))...  31.3 us
  transfers between devices with their start and end apart: 1, of which 1 were waited for; matrix products, arithmetic and copies ran while one was open for 0% of the time, Pallas kernels for 0%

profile of v1, /device:TPU:8, one launch (start us, length us, event | category | flops | bytes accessed | tf_op | source)
XLA Modules:
  0.0 1255.1 jit_solution(11155757264880645641)
XLA Ops:
  7.2 0.0 copy-start
  7.2 0.0 reduce-scatter.2.cloned.1.call-start
  7.2 1.6 slice.36
  8.8 1.5 slice.39
  10.3 0.9 slice.42
  11.2 1.4 bitcast_convert_fusion.3
  12.6 0.3 dynamic_update_slice.12
  12.9 13.2 %all-gather = bf16[256,512]{1,0:T(8,128)(2,1)S(1)} all-gather(bf16[32,512]{1,0:T(8,128)(2,1)S(1)} %convert_element_type.70), channel_id=2, replica_groups=mesh['rows'=64,'cols'=8] {'cols'}, dimensions={0}, use_global_device_ids=true | all-gather | bytes 294912 | tf_op jit(solution)/shard_map/all_gather | solution.py:30
  26.2 1.8 convolution_bitcast_fusion.4
  27.9 284.2 %all-reduce.4 = bf16[256,512]{0,1:T(8,128)(2,1)S(1)} all-reduce(f32[256,512]{0,1:T(8,128)} %convolution_bitcast_fusion.4), channel_id=1, replica_groups=mesh['rows'=64,'cols'=8] {'rows'}, use_global_device_ids=true, to_apply=%region_1.0 | all-reduce | flops 131072 | bytes 786432 | tf_op jit(solution)/shard_map/psum | solution.py:33
  312.1 0.9 dynamic_update_slice.13
  313.0 0.9 fusion.7
  314.0 0.0 copy-start.2
  314.0 13.9 %all-gather.1 = bf16[256,512]{1,0:T(8,128)(2,1)} all-gather(bf16[32,512]{1,0:T(8,128)(2,1)S(1)} %fusion.7), channel_id=3, replica_groups=mesh['rows'=64,'cols'=8] {'cols'}, dimensions={0}, use_global_device_ids=true | all-gather | bytes 294912 | tf_op jit(solution)/shard_map/all_gather | solution.py:30
  327.9 1.0 reduce_sum.49
  328.9 1.8 convolution_bitcast_fusion.3
  330.7 280.2 %all-reduce.5 = bf16[256,512]{0,1:T(8,128)(2,1)} all-reduce(f32[256,512]{0,1:T(8,128)} %convolution_bitcast_fusion.3), channel_id=1, replica_groups=mesh['rows'=64,'cols'=8] {'rows'}, use_global_device_ids=true, to_apply=%region_3.0 | all-reduce | flops 131072 | bytes 786432 | tf_op jit(solution)/shard_map/psum | solution.py:33
  610.9 0.0 copy-done.2
  610.9 0.6 copy.13
  611.5 0.9 dynamic_update_slice.14
  612.4 1.2 fusion.9
  613.6 13.9 %all-gather.2 = bf16[256,512]{1,0:T(8,128)(2,1)} all-gather(bf16[32,512]{1,0:T(8,128)(2,1)S(1)} %fusion.9), channel_id=4, replica_groups=mesh['rows'=64,'cols'=8] {'cols'}, dimensions={0}, use_global_device_ids=true | all-gather | bytes 294912 | tf_op jit(solution)/shard_map/all_gather | solution.py:30
  627.6 1.0 reduce_sum.50
  628.6 1.8 convolution_bitcast_fusion.2
  630.3 278.0 %all-reduce.6 = bf16[256,512]{0,1:T(8,128)(2,1)} all-reduce(f32[256,512]{0,1:T(8,128)} %convolution_bitcast_fusion.2), channel_id=1, replica_groups=mesh['rows'=64,'cols'=8] {'rows'}, use_global_device_ids=true, to_apply=%region_5.0 | all-reduce | flops 131072 | bytes 786432 | tf_op jit(solution)/shard_map/psum | solution.py:33
  908.3 0.3 dynamic_update_slice.15
  908.7 1.4 fusion.8
  910.0 13.9 %all-gather.3 = bf16[256,512]{1,0:T(8,128)(2,1)} all-gather(bf16[32,512]{1,0:T(8,128)(2,1)S(1)} %fusion.8), channel_id=5, replica_groups=mesh['rows'=64,'cols'=8] {'cols'}, dimensions={0}, use_global_device_ids=true | all-gather | bytes 294912 | tf_op jit(solution)/shard_map/all_gather | solution.py:30
  924.0 1.0 reduce_sum.51
  924.9 1.8 convolution_bitcast_fusion.1
  926.7 280.0 %all-reduce.7 = bf16[256,512]{0,1:T(8,128)(2,1)} all-reduce(f32[256,512]{0,1:T(8,128)} %convolution_bitcast_fusion.1), channel_id=1, replica_groups=mesh['rows'=64,'cols'=8] {'rows'}, use_global_device_ids=true, to_apply=%region_7.0 | all-reduce | flops 131072 | bytes 786432 | tf_op jit(solution)/shard_map/psum | solution.py:33
  1206.7 0.0 copy-done
  1206.7 4.1 fusion.1
  1210.8 0.0 reduce-scatter.2.cloned.1.call-update
  1210.8 2.2 pad_maximum_fusion
  1213.0 0.0 copy-start.1
  1213.0 2.3 copy.11
  1215.3 31.3 %reduce-scatter.2.cloned.1.call-done = bf16[64,1536]{1,0:T(8,128)(2,1)} async-done(((bf16[512,1536]{1,0:T(8,128)(2,1)}), bf16[64,1536]{1,0:T(8,128)(2,1)}) %reduce-scatter.2.cloned.1.call-update) | async-done | bytes 196624 | tf_op jit(solution)/shard_map/reduce_scatter | solution.py:38
  1246.6 0.0 copy-done.1
  1246.6 1.6 subtract_convert_fusion
  (7 shorter events, 0.1 us)
Async XLA Ops:
  7.2 1199.6 %copy-start = (bf16[1536,4,256]{2,1,0:T(4,128)(2,1)S(1)}, bf16[1536,4,256]{2,1,0:T(4,128)(2,1)}, u32[]{:S(2)}) copy-start(bf16[1536,4,256]{2,1,0:T(4,128)(2,1)} %param.6) | copy-start | bytes 9437188
  7.2 1239.5 %reduce-scatter.2.cloned.1.call-start = ((), (), s32[]{:S(2)}) async-start(), calls=%async_computation.1 | async-start | bytes 1769472 | tf_op jit(solution)/shard_map/reduce_scatter | solution.py:38
  314.0 296.9 %copy-start.2 = (bf16[1,32,2,256]{3,2,1,0:T(2,128)(2,1)S(1)}, bf16[1,32,2,256]{3,2,1,0:T(2,128)(2,1)}, u32[]{:S(2)}) copy-start(bf16[1,32,2,256]{3,2,1,0:T(2,128)(2,1)} %slice.39) | copy-start | bytes 98308
  1213.0 33.6 %copy-start.1 = (bf16[64,1536]{1,0:T(8,128)(2,1)S(1)}, bf16[64,1536]{1,0:T(8,128)(2,1)}, u32[]{:S(2)}) copy-start(bf16[64,1536]{1,0:T(8,128)(2,1)} %param.9) | copy-start | bytes 589828
Sparse Core Ops, SparseCore 0:
  1211.0 35.6 reduce-scatter.1
